TPU v7x, 32 devices: a whole 2x2x4 slice. The times are simulated.
32 devices in a mesh: shard: 8 (over z, x), rep: 4 (over y, core).
Axes of the slice: x: 2, y: 2, z: 4, core: 2. Of those that a mesh axis runs over, the one named last changes fastest.
Arguments:
- images: bfloat16 [32, 197, 768], P(('shard', 'rep')), may hold values from -6 to 6
- cotangent: bfloat16 [32, 197, 768], P(('shard', 'rep')), may hold values from -6 to 6
- weights_in: float32 [768, 6144], P('shard'), may hold values from -13 to 13
- weights_down: float32 [3072, 768], P('shard'), may hold values from -0.109375 to 0.109375
- vectors: float32 [12, 768], P(None, 'shard'), may hold values from -1.5 to 1.5, as said below
- mean_in: float32 [768, 6144], P('shard'), may hold values from -256 to 256
- mean_down: float32 [3072, 768], P('shard'), may hold values from -256 to 256
- mean_vectors: float32 [12, 768], P(None, 'shard'), may hold values from -256 to 256
- square_in: float32 [768, 6144], P('shard'), may hold values from 63.04 to 6304
- square_down: float32 [3072, 768], P('shard'), may hold values from 63.04 to 6304
- square_vectors: float32 [12, 768], P(None, 'shard'), may hold values from 63.04 to 6304
Outputs:
- block_out: bfloat16 [32, 197, 768], P(('shard', 'rep'))
- input_grad: float32 [32, 197, 768], P(('shard', 'rep'))
- grad_in: float32 [768, 6144], P('shard')
- grad_down: float32 [3072, 768], P('shard')
- grad_vectors: float32 [12, 768], P(None, 'shard')
- updated_in: float32 [768, 6144], P('shard')
- updated_down: float32 [3072, 768], P('shard')
- updated_vectors: float32 [12, 768], P(None, 'shard')
- next_mean_in: float32 [768, 6144], P('shard')
- next_mean_down: float32 [3072, 768], P('shard')
- next_mean_vectors: float32 [12, 768], P(None, 'shard')
- next_square_in: float32 [768, 6144], P('shard')
- next_square_down: float32 [3072, 768], P('shard')
- next_square_vectors: float32 [12, 768], P(None, 'shard')
Inputs may be any that keep to these rules, and one draw needn't show every extreme that they name: `vectors`: rows 0 and 5 are the norms' gains.
All inputs are finite; a program needn't handle non-finite values.
Results may differ from a plain program's by a relative error of at most 0.023.
Values may be sent and summed in bfloat16 or wider, within the bound.
A program may use at most 128 MiB of HBM per device.

v0:
```python
import math
import jax
import jax.numpy as jnp
from jax import lax
from jax.sharding import PartitionSpec as P

HEADS = 12
NORM_EPS = 1e-06
BETA_ONE = 0.9
BETA_TWO = 0.95
ADAM_EPS = 1e-08
RATE_MATRIX = 0.008
RATE_VECTOR = 0.15
DECAY_MATRIX = 0.05
STEP_COUNT = 2.0


def to_half(array_in):
    return array_in.astype(jnp.bfloat16)


def matmul(left, right):
    return jnp.dot(left, right, preferred_element_type=jnp.float32)


def times_transposed(left, right):
    return lax.dot_general(
        left, right, (((1,), (1,)), ((), ())), preferred_element_type=jnp.float32
    )


def transposed_times(left, right):
    return lax.dot_general(
        left, right, (((0,), (0,)), ((), ())), preferred_element_type=jnp.float32
    )


def layer_norm(inputs, gain, shift):
    centred = inputs - jnp.mean(inputs, axis=-1, keepdims=True)
    inv_std = lax.rsqrt(jnp.mean(centred * centred, axis=-1, keepdims=True) + NORM_EPS)
    normed = centred * inv_std
    return (normed, inv_std, normed * gain + shift)


def norm_back(grad_after, normed, inv_std, gain):
    grad_normed = grad_after * gain
    grad_inputs = inv_std * (
        grad_normed
        - jnp.mean(grad_normed, axis=-1, keepdims=True)
        - normed * jnp.mean(grad_normed * normed, axis=-1, keepdims=True)
    )
    return (grad_inputs, jnp.sum(grad_after * normed, axis=0), jnp.sum(grad_after, axis=0))


def gaussian_unit(hidden):
    cdf_part = 0.5 * (1.0 + jax.scipy.special.erf(hidden * 0.7071067811865476))
    slope = cdf_part + hidden * jnp.exp(-0.5 * hidden * hidden) * 0.3989422804014327
    return (hidden * cdf_part, slope)


def head_scores(query_heads, key_heads, score_scale):
    return (
        jnp.einsum("bqhe,bkhe->bhqk", query_heads, key_heads, preferred_element_type=jnp.float32)
        * score_scale
    )


def forward_pass(images, matrix_half, down_half, vector_half):
    img_count, seq_len, model_width = images.shape
    head_dim = model_width // HEADS
    score_scale = 1.0 / math.sqrt(head_dim)
    row_count = img_count * seq_len
    head_shape = (img_count, seq_len, HEADS, head_dim)
    vector_float = vector_half.astype(jnp.float32)
    flat_in = images.reshape(row_count, model_width).astype(jnp.float32)
    normed_one, inv_one, pre_one = layer_norm(flat_in, vector_float[0], vector_float[1])
    act_one = to_half(pre_one)
    projected = matmul(act_one, matrix_half[:, : 3 * model_width])
    query_heads = to_half(projected[:, :model_width] + vector_float[2]).reshape(head_shape)
    key_heads = to_half(projected[:, model_width : 2 * model_width]).reshape(head_shape)
    value_heads = to_half(projected[:, 2 * model_width :] + vector_float[3]).reshape(head_shape)
    scores = head_scores(query_heads, key_heads, score_scale)
    log_total = jax.nn.logsumexp(scores, axis=-1, keepdims=True)
    probs_half = to_half(jnp.exp(scores - log_total))
    attended = to_half(
        jnp.einsum(
            "bhqk,bkhe->bqhe", probs_half, value_heads, preferred_element_type=jnp.float32
        ).reshape(row_count, model_width)
    )
    hidden_one = (
        flat_in
        + matmul(attended, matrix_half[:, 3 * model_width : 4 * model_width])
        + vector_float[4]
    )
    normed_two, inv_two, pre_two = layer_norm(hidden_one, vector_float[5], vector_float[6])
    act_two = to_half(pre_two)
    up_input = matmul(act_two, matrix_half[:, 4 * model_width :]) + vector_float[8:].reshape(-1)
    gelu_out, gelu_slope = gaussian_unit(up_input)
    gelu_half = to_half(gelu_out)
    block_out = to_half(hidden_one + matmul(gelu_half, down_half) + vector_float[7])
    saved = (
        normed_one,
        inv_one,
        act_one,
        query_heads,
        key_heads,
        value_heads,
        log_total,
        attended,
        normed_two,
        inv_two,
        act_two,
        gelu_slope,
        gelu_half,
    )
    return (block_out.reshape(images.shape), saved)


def backward_pass(cotangent, saved, matrix_half, down_half, vector_half):
    (
        normed_one,
        inv_one,
        act_one,
        query_heads,
        key_heads,
        value_heads,
        log_total,
        attended,
        normed_two,
        inv_two,
        act_two,
        gelu_slope,
        gelu_half,
    ) = saved
    img_count, seq_len, model_width = cotangent.shape
    head_dim = model_width // HEADS
    score_scale = 1.0 / math.sqrt(head_dim)
    row_count = img_count * seq_len
    head_shape = (img_count, seq_len, HEADS, head_dim)
    vector_float = vector_half.astype(jnp.float32)
    joint_weights = matrix_half[:, : 3 * model_width]
    output_weights = matrix_half[:, 3 * model_width : 4 * model_width]
    upward_weights = matrix_half[:, 4 * model_width :]
    grad_half = cotangent.reshape(row_count, model_width)
    grad_out = grad_half.astype(jnp.float32)
    grad_up = times_transposed(grad_half, down_half) * gelu_slope
    up_half = to_half(grad_up)
    grad_act_two = times_transposed(up_half, upward_weights)
    grad_norm_two, grad_gain_two, grad_shift_two = norm_back(
        grad_act_two, normed_two, inv_two, vector_float[5]
    )
    grad_hidden = grad_out + grad_norm_two
    hidden_half = to_half(grad_hidden)
    grad_att = to_half(times_transposed(hidden_half, output_weights)).reshape(head_shape)
    prob_float = jnp.exp(head_scores(query_heads, key_heads, score_scale) - log_total)
    probs_half = to_half(prob_float)
    grad_probs = jnp.einsum(
        "bqhe,bkhe->bhqk", grad_att, value_heads, preferred_element_type=jnp.float32
    )
    row_inner = jnp.sum(prob_float * grad_probs, axis=-1, keepdims=True)
    grad_scores = to_half(prob_float * (grad_probs - row_inner) * score_scale)
    grad_query = jnp.einsum(
        "bhqk,bkhe->bqhe", grad_scores, key_heads, preferred_element_type=jnp.float32
    ).reshape(row_count, model_width)
    grad_key = jnp.einsum(
        "bhqk,bqhe->bkhe", grad_scores, query_heads, preferred_element_type=jnp.float32
    ).reshape(row_count, model_width)
    grad_value = jnp.einsum(
        "bhqk,bqhe->bkhe", probs_half, grad_att, preferred_element_type=jnp.float32
    ).reshape(row_count, model_width)
    grad_proj = to_half(jnp.concatenate([grad_query, grad_key, grad_value], axis=1))
    grad_act_one = times_transposed(grad_proj, joint_weights)
    grad_norm_one, grad_gain_one, grad_shift_one = norm_back(
        grad_act_one, normed_one, inv_one, vector_float[0]
    )
    input_grad = (grad_hidden + grad_norm_one).reshape(cotangent.shape)
    grad_down = transposed_times(gelu_half, grad_half)
    small_rows = jnp.stack(
        [
            grad_gain_one,
            grad_shift_one,
            jnp.sum(grad_query, axis=0),
            jnp.sum(grad_value, axis=0),
            jnp.sum(grad_hidden, axis=0),
            grad_gain_two,
            grad_shift_two,
            jnp.sum(grad_out, axis=0),
        ]
    )
    grad_vectors = jnp.concatenate(
        [small_rows, jnp.sum(grad_up, axis=0).reshape(4, model_width)], axis=0
    )
    factors = (act_one, grad_proj, attended, hidden_half, act_two, up_half)
    return (input_grad, grad_down, grad_vectors, factors)


def adam_update(weights, first, second, gradient, rate, decay):
    next_first = BETA_ONE * first + (1.0 - BETA_ONE) * gradient
    next_second = BETA_TWO * second + (1.0 - BETA_TWO) * gradient * gradient
    corr_first = next_first / (1.0 - BETA_ONE**STEP_COUNT)
    corr_second = next_second / (1.0 - BETA_TWO**STEP_COUNT)
    updated = weights - rate * (corr_first / (jnp.sqrt(corr_second) + ADAM_EPS) + decay * weights)
    return (updated, next_first, next_second)


def local(
    images,
    cotangent,
    weights_in,
    weights_down,
    vectors,
    mean_in,
    mean_down,
    mean_vectors,
    square_in,
    square_down,
    square_vectors,
):
    halves = (to_half(weights_in), to_half(weights_down), to_half(vectors))
    forward_set = (
        lax.all_gather(halves[0], "shard", axis=0, tiled=True),
        lax.all_gather(halves[1], "shard", axis=0, tiled=True),
        lax.all_gather(halves[2], "shard", axis=1, tiled=True),
    )
    block_out, saved = forward_pass(images, forward_set[0], forward_set[1], forward_set[2])
    backward_set = (
        lax.all_gather(halves[0], "shard", axis=0, tiled=True),
        lax.all_gather(halves[1], "shard", axis=0, tiled=True),
        lax.all_gather(halves[2], "shard", axis=1, tiled=True),
    )
    input_grad, grad_down_local, grad_vectors_local, factors = backward_pass(
        cotangent, saved, backward_set[0], backward_set[1], backward_set[2]
    )
    act_one, grad_proj, attended, hidden_half, act_two, up_half = factors

    def column_part(activation, gradient):
        return transposed_times(activation, gradient)

    owned_in = lax.psum_scatter(
        jnp.concatenate(
            [
                column_part(act_one, grad_proj),
                column_part(attended, hidden_half),
                column_part(act_two, up_half),
            ],
            axis=1,
        ).astype(jnp.bfloat16),
        "shard",
        scatter_dimension=0,
        tiled=True,
    )
    owned_down, owned_vectors = (
        lax.psum_scatter(
            grad_down_local.astype(jnp.bfloat16), "shard", scatter_dimension=0, tiled=True
        ).astype(jnp.float32),
        lax.psum_scatter(
            grad_vectors_local.astype(jnp.bfloat16), "shard", scatter_dimension=1, tiled=True
        ).astype(jnp.float32),
    )
    grad_in, grad_down, grad_vectors = (
        lax.psum(owned_in, "rep").astype(jnp.float32),
        lax.psum(owned_down.astype(jnp.bfloat16), "rep").astype(jnp.float32),
        lax.psum(owned_vectors.astype(jnp.bfloat16), "rep").astype(jnp.float32),
    )
    new_in = adam_update(weights_in, mean_in, square_in, grad_in, RATE_MATRIX, DECAY_MATRIX)
    new_down = adam_update(
        weights_down, mean_down, square_down, grad_down, RATE_MATRIX, DECAY_MATRIX
    )
    new_vectors = adam_update(vectors, mean_vectors, square_vectors, grad_vectors, RATE_VECTOR, 0.0)
    return (
        block_out,
        input_grad,
        grad_in,
        grad_down,
        grad_vectors,
        new_in[0],
        new_down[0],
        new_vectors[0],
        new_in[1],
        new_down[1],
        new_vectors[1],
        new_in[2],
        new_down[2],
        new_vectors[2],
    )


def solution(mesh):
    placed = (
        P(("shard", "rep"), None, None),
        P(("shard", "rep"), None, None),
        P("shard", None),
        P("shard", None),
        P(None, "shard"),
        P("shard", None),
        P("shard", None),
        P(None, "shard"),
        P("shard", None),
        P("shard", None),
        P(None, "shard"),
    )
    return jax.shard_map(
        local,
        mesh=mesh,
        in_specs=placed,
        out_specs=(
            P(("shard", "rep"), None, None),
            P(("shard", "rep"), None, None),
            P("shard", None),
            P("shard", None),
            P(None, "shard"),
            P("shard", None),
            P("shard", None),
            P(None, "shard"),
            P("shard", None),
            P("shard", None),
            P(None, "shard"),
            P("shard", None),
            P("shard", None),
            P(None, "shard"),
        ),
        check_vma=False,
    )
```

profile of v0, /device:TPU:0, one launch (start us, length us, event | category | flops | bytes accessed | tf_op | source)
XLA Modules:
  0.0 623.4 jit_solution(6696602671923517766)
XLA Ops:
  7.2 2.9 convert_element_type.95
  10.2 0.0 all-gather.6.cloned.1.call-start
  10.2 0.9 convert_element_type.105
  11.2 33.3 %all-gather = bf16[8,96,12]{1,2,0:T(8,128)(2,1)S(1)} all-gather(bf16[1,96,12]{1,2,0:T(8,128)(2,1)S(1)} %convert_bitcast_fusion.1), channel_id=1, replica_groups=mesh['shard'=8,'rep'=4] {'shard'}, dimensions={0}, use_global_device_ids=true | all-gather | bytes 20736 | tf_op jit(solution)/shard_map/all_gather | solution.py:223
  44.5 0.1 reshape.207
  44.6 0.1 slice_reduce_fusion
  44.7 0.1 convert_reduce_fusion
  44.8 0.2 fusion.57
  45.1 105.8 %all-gather.4.cloned.1.call-done = bf16[768,6144]{1,0:T(8,128)(2,1)} async-done(((bf16[96,6144]{1,0:T(8,128)(2,1)}), bf16[768,6144]{1,0:T(8,128)(2,1)}) %all-gather.4.cloned.1.call-update) | async-done | bytes 9437200 | tf_op jit(solution)/shard_map/all_gather | solution.py:221
  150.9 3.0 fusion.10
  153.9 0.1 fusion.58
  154.0 0.9 copy.63
  154.9 0.2 copy.64
  155.1 0.2 copy.62
  155.3 1.5 multiply_reduce_fusion.1
  156.9 0.5 exponential_reduce_fusion
  157.4 0.6 convolution_convert_fusion.4
  158.0 2.0 fusion.87
  160.0 0.2 multiply_reduce_fusion.4
  160.3 5.4 multiply_convert_fusion.1
  165.7 1.0 copy-done.7
  166.7 3.7 convolution_convert_fusion
  170.4 0.2 reduce-scatter.6.cloned.1.call-start
  170.7 60.5 %all-gather.6.cloned.1.call-done = bf16[3072,768]{1,0:T(8,128)(2,1)} async-done(((bf16[384,768]{1,0:T(8,128)(2,1)}), bf16[3072,768]{1,0:T(8,128)(2,1)}) %all-gather.6.cloned.1.call-update) | async-done | bytes 4718608 | tf_op jit(solution)/shard_map/all_gather | solution.py:222
  231.2 5.0 fusion.90
  236.2 4.7 multiply_reduce_fusion.2
  240.9 1.4 fusion.84
  242.3 2.5 convolution_convert_fusion.5
  244.8 1.9 copy.66
  246.7 2.5 convolution_convert_fusion.3
  249.2 2.4 copy.70
  251.6 3.0 fusion.91
  254.6 4.7 fusion.30
  259.3 4.9 fusion.86
  264.2 0.7 fusion.85
  264.9 0.7 copy-done.23
  265.6 1.3 convolution_convert_fusion.2
  267.0 0.1 copy-done.21
  267.1 1.6 convolution_convert_fusion.1
  268.7 4.2 pad_maximum_fusion
  272.9 0.3 reduce-scatter.10.cloned.1.call-start
  273.2 0.7 copy-done.15
  273.9 0.1 reduce.9
  274.0 0.1 stack.35
  274.1 0.1 stack.34
  274.2 0.0 copy-done.29
  274.2 0.1 copy-done.31
  274.3 3.6 fusion.56
  277.9 0.1 concatenate.14
  278.0 0.8 copy.76
  278.9 50.0 %reduce-scatter.8.cloned.1.call-done = bf16[384,768]{1,0:T(8,128)(2,1)} async-done(((bf16[3072,768]{1,0:T(8,128)(2,1)}), bf16[384,768]{1,0:T(8,128)(2,1)}) %reduce-scatter.8.cloned.1.call-update) | async-done | bytes 589840 | tf_op jit(solution)/shard_map/reduce_scatter | solution.py:253
  328.9 165.2 %reduce-scatter.6.cloned.1.call-done = bf16[96,6144]{1,0:T(8,128)(2,1)} async-done(((bf16[768,6144]{1,0:T(8,128)(2,1)}), bf16[96,6144]{1,0:T(8,128)(2,1)}) %reduce-scatter.6.cloned.1.call-update) | async-done | bytes 1179664 | tf_op jit(solution)/shard_map/reduce_scatter | solution.py:239
  494.2 0.3 fusion.55
  494.4 1.4 copy.71
  495.9 4.3 fusion.37
  500.2 58.6 %reduce-scatter.10.cloned.1.call-done = bf16[96,12]{1,0:T(8,128)(2,1)} async-done(((bf16[768,12]{1,0:T(8,128)(2,1)}), bf16[96,12]{1,0:T(8,128)(2,1)}) %reduce-scatter.10.cloned.1.call-update) | async-done | bytes 2320
  558.8 0.8 copy.77
  559.6 5.7 psum.23
  565.3 0.6 multiply_subtract_fusion.2
  565.9 40.4 %all-reduce.3.cloned.1.call-done = (bf16[96,6144]{1,0:T(8,128)(2,1)}, bf16[384,768]{1,0:T(8,128)(2,1)}) async-done(((bf16[96,6144]{1,0:T(8,128)(2,1)}, bf16[384,768]{1,0:T(8,128)(2,1)}), (bf16[96,6144]{1,0:T(8,128)(2,1)}, bf16[384,768]{1,0:T(8,128)(2,1)})) %all-reduce.3.cloned.1.call-update) | async-done | bytes 1769488 | tf_op jit(solution)/shard_map/psum | solution.py:261
  606.3 4.6 multiply_subtract_fusion.1
  610.9 1.1 copy-done.17
  612.0 0.3 copy-done.22
  612.3 4.3 multiply_subtract_fusion
  (86 shorter events, 0.5 us)
Async XLA Ops:
  7.2 3.0 copy-start.3
  7.2 143.7 %all-gather.4.cloned.1.call-start = ((), (), s32[]{:S(2)}) async-start(), calls=%async_computation.3 | async-start | bytes 10616832 | tf_op jit(solution)/shard_map/all_gather | solution.py:221
  10.1 1.0 copy-start.25
  10.1 34.5 %copy-start.9 = (bf16[1,197,768]{2,1,0:T(8,128)(2,1)S(1)}, bf16[1,197,768]{2,1,0:T(8,128)(2,1)}, u32[]{:S(2)}) copy-start(bf16[1,197,768]{2,1,0:T(8,128)(2,1)} %param.11) | copy-start | bytes 907780
  10.2 221.0 %all-gather.6.cloned.1.call-start = ((), (), s32[]{:S(2)}) async-start(), calls=%async_computation.4 | async-start | bytes 5308416 | tf_op jit(solution)/shard_map/all_gather | solution.py:222
  11.1 317.8 %reduce-scatter.8.cloned.1.call-start = ((), (), s32[]{:S(2)}) async-start(), calls=%async_computation.6 | async-start | bytes 5308416 | tf_op jit(solution)/shard_map/reduce_scatter | solution.py:253
  155.1 2.2 copy-start.18
  156.8 1.1 copy-start.10
  158.0 2.3 copy-start.19
  160.0 76.2 %copy-start.1 = (f32[197,768]{1,0:T(8,128)}, f32[197,768]{1,0:T(8,128)S(1)}, u32[]{:S(2)}) copy-start(f32[197,768]{1,0:T(8,128)S(1)} %get-tuple-element.111) | copy-start | bytes 1815556
  160.3 6.4 %copy-start.13 = (bf16[1,197,768]{2,1,0:T(8,128)(2,1)S(1)}, bf16[1,197,768]{2,1,0:T(8,128)(2,1)}, u32[]{:S(2)}) copy-start(bf16[1,197,768]{2,1,0:T(8,128)(2,1)} %param.12) | copy-start | bytes 907780
  165.7 1.0 copy-start.7
  170.4 323.7 %reduce-scatter.6.cloned.1.call-start = ((), (), s32[]{:S(2)}) async-start(), calls=%async_computation.5 | async-start | bytes 10616832 | tf_op jit(solution)/shard_map/reduce_scatter | solution.py:239
  236.2 4.7 copy-start.20
  236.2 4.7 copy-start.14
  259.3 4.9 copy-start.6
  264.1 1.5 copy-start.11
  264.1 1.5 copy-start.28
  264.1 1.5 copy-start.30
  264.8 0.8 copy-start.23
  265.6 1.3 copy-start.2
  265.6 1.5 copy-start.21
  267.1 1.6 copy-start.5
  272.9 1.0 copy-start.15
  272.9 1.3 copy-start.12
  272.9 1.3 copy-start.24
  272.9 1.3 copy-start.29
  272.9 1.4 copy-start.31
  272.9 285.9 %reduce-scatter.10.cloned.1.call-start = ((), (), s32[]{:S(2)}) async-start(), calls=%async_computation.7 | async-start | bytes 221184
  278.9 327.5 %all-reduce.3.cloned.1.call-start = ((), (), s32[]{:S(2)}) async-start(), calls=%async_computation.8 | async-start | bytes 3538944 | tf_op jit(solution)/shard_map/psum | solution.py:261
  494.2 1.7 copy-start.8
  495.9 69.4 %copy-start.26 = (f32[12,96]{1,0:T(8,128)S(1)}, f32[12,96]{1,0:T(8,128)}, u32[]{:S(2)}) copy-start(f32[12,96]{1,0:T(8,128)} %param.18) | copy-start | bytes 13828
  495.9 69.4 %copy-start.27 = (f32[12,96]{1,0:T(8,128)S(1)}, f32[12,96]{1,0:T(8,128)}, u32[]{:S(2)}) copy-start(f32[12,96]{1,0:T(8,128)} %param.21) | copy-start | bytes 13828
  495.9 110.4 %copy-start.4 = (f32[384,768]{1,0:T(8,128)S(1)}, f32[384,768]{1,0:T(8,128)}, u32[]{:S(2)}) copy-start(f32[384,768]{1,0:T(8,128)} %param.14) | copy-start | bytes 3538948
  606.3 4.6 copy-start
  606.3 4.6 copy-start.16
  606.3 5.7 copy-start.17
  606.3 5.9 copy-start.22
Sparse Core Ops, SparseCore 0:
  10.8 140.0 all-gather.3
  153.6 77.5 all-gather.5
  234.9 94.0 reduce-scatter.7
  332.3 161.7 reduce-scatter.5
  497.8 60.9 reduce-scatter.9
  561.2 45.0 all-reduce.2
where the time goes:
time: 624 us; the launch traced here: 623 us
  waiting for transfers between devices  481 us (77%)
  matrix products  54.9 us (9%)
  blocking collectives  38.9 us (6%)
  other arithmetic  20.4 us (3%)
  between operations  14.6 us (2%)
  local copies, waits for them, and re-layouts  13.3 us (2%)
    reduce_scatter x1, waiting for transfers between devices, local(): lax.psum_scatter(jnp.concatenate([column_part(act_one, grad_proj), column...  165 us
    all_gather x1, waiting for transfers between devices, local(): lax.all_gather(halves[0], 'shard', axis=0, tiled=True)  106 us
    all_gather x1, waiting for transfers between devices, local(): lax.all_gather(halves[1], 'shard', axis=0, tiled=True)  60.5 us
    unnamed x7, waiting for transfers between devices  58.7 us
    reduce_scatter x1, waiting for transfers between devices, local(): lax.psum_scatter(grad_down_local.astype(jnp.bfloat16), 'shard', scatter_d...  50 us
    psum x1, waiting for transfers between devices, local(): lax.psum(owned_in, 'rep').astype(jnp.float32)  40.4 us
    all_gather x1, blocking collectives, local(): lax.all_gather(halves[2], 'shard', axis=1, tiled=True)  33.3 us
    dot_general x4, matrix products, times_transposed(): lax.dot_general(left, right, (((1,), (1,)), ((), ())), preferred_element_...  15.7 us
  transfers between devices with their start and end apart: 6, of which 6 were waited for; matrix products, arithmetic and copies ran while one was open for 12% of the time, Pallas kernels for 0%

commit v1 on v0

--- a/solution.py
+++ b/solution.py
@@ -258,7 +258,7 @@
         ).astype(jnp.float32),
     )
     grad_in, grad_down, grad_vectors = (
-        lax.psum(owned_in, "rep").astype(jnp.float32),
+        jnp.sum(lax.all_gather(owned_in, "rep"), axis=0).astype(jnp.float32),
         lax.psum(owned_down.astype(jnp.bfloat16), "rep").astype(jnp.float32),
         lax.psum(owned_vectors.astype(jnp.bfloat16), "rep").astype(jnp.float32),
     )

time: 624 us -> 710 us (1.14)
  waiting for transfers between devices: 481 us -> 559 us
  other arithmetic: 20.4 us -> 28.3 us
    reduce_scatter x1, waiting for transfers between devices: 50 us -> 94 us  [local(): lax.psum_scatter(grad_down_local.astype(jnp.bfloat16), 'shard', scatter_d...]
    all_gather x0 -> x1, waiting for transfers between devices: none -> 31 us  [local(): lax.all_gather(owned_in, 'rep')]
    all_gather x1, waiting for transfers between devices: 60.5 us -> 79.2 us  [local(): lax.all_gather(halves[1], 'shard', axis=0, tiled=True)]
    reduce_scatter x1, waiting for transfers between devices: 165 us -> 154 us  [local(): lax.psum_scatter(jnp.concatenate([column_part(act_one, grad_proj), column...]
    unnamed x7 -> x8, waiting for transfers between devices: 58.7 us -> 57.8 us
  transfers between devices with their start and end apart: 6 -> 7, of which waited for: 6 -> 7; matrix products, arithmetic and copies ran while one was open for 12% -> 2% of each run, Pallas kernels for 0% -> 0%
where the time goes in v1:
time: 710 us; the launch traced here: 709 us
  waiting for transfers between devices  559 us (79%)
  matrix products  59 us (8%)
  blocking collectives  38.9 us (5%)
  other arithmetic  28.3 us (4%)
  between operations  14.5 us (2%)
  local copies, waits for them, and re-layouts  9.41 us (1%)
    reduce_scatter x1, waiting for transfers between devices, local(): lax.psum_scatter(jnp.concatenate([column_part(act_one, grad_proj), column...  154 us
    all_gather x1, waiting for transfers between devices, local(): lax.all_gather(halves[0], 'shard', axis=0, tiled=True)  107 us
    reduce_scatter x1, waiting for transfers between devices, local(): lax.psum_scatter(grad_down_local.astype(jnp.bfloat16), 'shard', scatter_d...  94 us
    all_gather x1, waiting for transfers between devices, local(): lax.all_gather(halves[1], 'shard', axis=0, tiled=True)  79.2 us
    unnamed x8, waiting for transfers between devices  57.8 us
    psum x1, waiting for transfers between devices, local(): lax.psum(owned_down.astype(jnp.bfloat16), 'rep').astype(jnp.float32)  35.8 us
    all_gather x1, blocking collectives, local(): lax.all_gather(halves[2], 'shard', axis=1, tiled=True)  33.3 us
    all_gather x1, waiting for transfers between devices, local(): lax.all_gather(owned_in, 'rep')  31 us
  transfers between devices with their start and end apart: 7, of which 7 were waited for; matrix products, arithmetic and copies ran while one was open for 2% of the time, Pallas kernels for 0%

profile of v1, /device:TPU:0, one launch (start us, length us, event | category | flops | bytes accessed | tf_op | source)
XLA Modules:
  0.0 709.5 jit_solution(15424044921802629227)
XLA Ops:
  7.2 2.8 convert_element_type.97
  10.1 0.0 reduce-scatter.8.cloned.1.call-start
  10.2 33.3 %all-gather.1 = bf16[8,96,12]{1,2,0:T(8,128)(2,1)S(1)} all-gather(bf16[1,96,12]{1,2,0:T(8,128)(2,1)S(1)} %convert_bitcast_fusion.1), channel_id=1, replica_groups=mesh['shard'=8,'rep'=4] {'shard'}, dimensions={0}, use_global_device_ids=true | all-gather | bytes 20736 | tf_op jit(solution)/shard_map/all_gather | solution.py:223
  43.5 0.1 reshape.208
  43.6 0.1 slice_reduce_fusion
  43.7 0.1 convert_reduce_fusion
  43.8 0.2 fusion.57
  44.0 106.9 %all-gather.6.cloned.1.call-done = bf16[768,6144]{1,0:T(8,128)(2,1)} async-done(((bf16[96,6144]{1,0:T(8,128)(2,1)}), bf16[768,6144]{1,0:T(8,128)(2,1)}) %all-gather.6.cloned.1.call-update) | async-done | bytes 9437200 | tf_op jit(solution)/shard_map/all_gather | solution.py:221
  151.0 3.0 fusion.10
  154.0 0.1 fusion.58
  154.1 0.2 copy.62
  154.3 0.9 copy.63
  155.2 0.2 copy.64
  155.4 1.7 multiply_reduce_fusion.1
  157.1 0.5 exponential_reduce_fusion
  157.6 0.6 convolution_convert_fusion.4
  158.2 2.0 fusion.87
  160.2 0.2 multiply_reduce_fusion.4
  160.4 5.2 multiply_convert_fusion.1
  165.7 1.0 copy-done.5
  166.7 3.7 convolution_convert_fusion
  170.4 0.0 all-reduce.2.cloned.1.call-start
  170.5 94.0 %reduce-scatter.8.cloned.1.call-done = bf16[384,768]{1,0:T(8,128)(2,1)} async-done(((bf16[3072,768]{1,0:T(8,128)(2,1)}), bf16[384,768]{1,0:T(8,128)(2,1)}) %reduce-scatter.8.cloned.1.call-update) | async-done | bytes 589840 | tf_op jit(solution)/shard_map/reduce_scatter | solution.py:253
  264.5 35.8 %all-reduce.2.cloned.1.call-done = bf16[384,768]{1,0:T(8,128)(2,1)} async-done(((bf16[384,768]{1,0:T(8,128)(2,1)}), bf16[384,768]{1,0:T(8,128)(2,1)}) %all-reduce.2.cloned.1.call-update) | async-done | bytes 589840 | tf_op jit(solution)/shard_map/psum | solution.py:262
  300.3 5.1 multiply_subtract_fusion.1
  305.4 0.2 reduce-scatter.6.cloned.1.call-start
  305.7 79.2 %all-gather.8.cloned.1.call-done = bf16[3072,768]{1,0:T(8,128)(2,1)} async-done(((bf16[384,768]{1,0:T(8,128)(2,1)}), bf16[3072,768]{1,0:T(8,128)(2,1)}) %all-gather.8.cloned.1.call-update) | async-done | bytes 4718608 | tf_op jit(solution)/shard_map/all_gather | solution.py:222
  384.9 5.0 fusion.90
  389.9 4.7 multiply_reduce_fusion.2
  394.6 1.4 fusion.84
  396.0 2.5 convolution_convert_fusion.5
  398.5 1.9 copy.66
  400.4 2.4 fusion.85
  402.9 2.0 fusion.91
  404.8 4.7 fusion.30
  409.5 4.5 fusion.86
  414.0 5.3 convolution_convert_fusion.1
  419.4 0.5 convolution_convert_fusion.3
  419.9 0.6 copy.70
  420.6 2.7 convolution_convert_fusion.2
  423.3 4.1 pad_maximum_fusion
  427.5 0.3 reduce-scatter.10.cloned.1.call-start
  427.8 0.7 copy-done.12
  428.4 0.1 reduce.10
  428.5 0.0 copy-done.18
  428.5 0.1 copy-done.22
  428.7 0.1 copy-done.23
  428.8 4.2 fusion.56
  433.0 0.1 stack.34
  433.1 0.1 stack.35
  433.2 0.1 concatenate.14
  433.3 0.8 copy.76
  434.2 0.0 all-gather.10.cloned.1.call-start
  434.2 153.9 %reduce-scatter.6.cloned.1.call-done = bf16[96,6144]{1,0:T(8,128)(2,1)} async-done(((bf16[768,6144]{1,0:T(8,128)(2,1)}), bf16[96,6144]{1,0:T(8,128)(2,1)}) %reduce-scatter.6.cloned.1.call-update) | async-done | bytes 1179664 | tf_op jit(solution)/shard_map/reduce_scatter | solution.py:239
  588.2 1.3 fusion.55
  589.5 1.4 copy.71
  591.0 4.2 fusion.37
  595.2 57.7 %reduce-scatter.10.cloned.1.call-done = bf16[96,12]{1,0:T(8,128)(2,1)} async-done(((bf16[768,12]{1,0:T(8,128)(2,1)}), bf16[96,12]{1,0:T(8,128)(2,1)}) %reduce-scatter.10.cloned.1.call-update) | async-done | bytes 2320
  652.9 0.8 copy.77
  653.7 5.7 psum.15
  659.4 0.6 multiply_subtract_fusion.2
  660.0 31.0 %all-gather.10.cloned.1.call-done = bf16[384,6144]{1,0:T(8,128)(2,1)} async-done(((bf16[96,6144]{1,0:T(8,128)(2,1)}), bf16[384,6144]{1,0:T(8,128)(2,1)}) %all-gather.10.cloned.1.call-update) | async-done | bytes 4718608 | tf_op jit(solution)/shard_map/all_gather | solution.py:261
  691.0 4.7 reduce_sum.193
  695.6 7.0 multiply_subtract_fusion
  (73 shorter events, 0.4 us)
Async XLA Ops:
  7.2 3.0 copy-start.19
  7.2 36.5 %copy-start.7 = (bf16[1,197,768]{2,1,0:T(8,128)(2,1)S(1)}, bf16[1,197,768]{2,1,0:T(8,128)(2,1)}, u32[]{:S(2)}) copy-start(bf16[1,197,768]{2,1,0:T(8,128)(2,1)} %param.11) | copy-start | bytes 907780
  7.2 143.8 %all-gather.6.cloned.1.call-start = ((), (), s32[]{:S(2)}) async-start(), calls=%async_computation.3 | async-start | bytes 10616832 | tf_op jit(solution)/shard_map/all_gather | solution.py:221
  10.1 254.3 %reduce-scatter.8.cloned.1.call-start = ((), (), s32[]{:S(2)}) async-start(), calls=%async_computation.6 | async-start | bytes 5308416 | tf_op jit(solution)/shard_map/reduce_scatter | solution.py:253
  155.3 2.2 copy-start.13
  157.1 1.1 copy-start.8
  158.2 2.2 copy-start.15
  160.2 229.7 %copy-start.2 = (f32[197,768]{1,0:T(8,128)}, f32[197,768]{1,0:T(8,128)S(1)}, u32[]{:S(2)}) copy-start(f32[197,768]{1,0:T(8,128)S(1)} %get-tuple-element.110) | copy-start | bytes 1815556
  160.4 6.3 copy-start.10
  165.7 1.0 copy-start.5
  170.4 129.9 %all-reduce.2.cloned.1.call-start = ((), (), s32[]{:S(2)}) async-start(), calls=%async_computation.7 | async-start | bytes 1179648 | tf_op jit(solution)/shard_map/psum | solution.py:262
  264.5 120.4 %all-gather.8.cloned.1.call-start = ((), (), s32[]{:S(2)}) async-start(), calls=%async_computation.4 | async-start | bytes 5308416 | tf_op jit(solution)/shard_map/all_gather | solution.py:222
  305.4 282.7 %reduce-scatter.6.cloned.1.call-start = ((), (), s32[]{:S(2)}) async-start(), calls=%async_computation.5 | async-start | bytes 10616832 | tf_op jit(solution)/shard_map/reduce_scatter | solution.py:239
  389.9 4.7 copy-start.17
  389.9 4.7 copy-start.11
  400.4 2.5 copy-start.4
  404.8 4.7 copy-start.14
  414.0 5.3 copy-start.16
  419.4 1.2 copy-start.9
  420.6 2.7 copy-start
  427.4 1.0 copy-start.12
  427.4 1.1 copy-start.18
  427.4 1.2 copy-start.22
  427.4 1.3 copy-start.23
  427.5 225.4 %reduce-scatter.10.cloned.1.call-start = ((), (), s32[]{:S(2)}) async-start(), calls=%async_computation.9 | async-start | bytes 221184
  433.3 157.7 %copy-start.3 = (f32[197,768]{1,0:T(8,128)S(1)}, f32[197,768]{1,0:T(8,128)}, u32[]{:S(2)}) copy-start(f32[197,768]{1,0:T(8,128)} %copy-done.2) | copy-start | bytes 1815556
  433.3 157.7 %copy-start.6 = (bf16[197,3072]{1,0:T(8,128)(2,1)S(1)}, bf16[197,3072]{1,0:T(8,128)(2,1)}, u32[]{:S(2)}) copy-start(bf16[197,3072]{1,0:T(8,128)(2,1)} %copy-done.5) | copy-start | bytes 3631108
  434.2 256.8 %all-gather.10.cloned.1.call-start = ((), (), s32[]{:S(2)}) async-start(), calls=%async_computation.8 | async-start | bytes 5898240 | tf_op jit(solution)/shard_map/all_gather | solution.py:261
  590.9 68.4 %copy-start.20 = (f32[12,96]{1,0:T(8,128)S(1)}, f32[12,96]{1,0:T(8,128)}, u32[]{:S(2)}) copy-start(f32[12,96]{1,0:T(8,128)} %param.18) | copy-start | bytes 13828
  590.9 68.4 %copy-start.21 = (f32[12,96]{1,0:T(8,128)S(1)}, f32[12,96]{1,0:T(8,128)}, u32[]{:S(2)}) copy-start(f32[12,96]{1,0:T(8,128)} %param.21) | copy-start | bytes 13828
  691.0 4.7 copy-start.1
Sparse Core Ops, SparseCore 0:
  10.8 140.1 all-gather.5
  170.6 93.8 reduce-scatter.7
  266.8 33.4 all-reduce.1
  305.6 79.3 all-gather.7
  427.6 160.4 reduce-scatter.5
  591.8 61.0 reduce-scatter.9
  654.4 36.4 all-gather.9
